TPU v7x, 32 devices: a whole 2x2x4 slice. The times are simulated.
32 devices in a mesh: dp: 8 (over z, y), mp: 4 (over x, core).
Axes of the slice: x: 2, y: 2, z: 4, core: 2. Of those that a mesh axis runs over, the one named last changes fastest.
Arguments:
- tokens: bfloat16 [8192, 2048], P('dp'), may hold values from -6 to 6
- out_cot: bfloat16 [8192, 2048], P('dp'), may hold values from -23 to 23
- lengths: int32 [8], P('dp'), may hold values from 1 to 1024, 6144 in all
- seq_family: int32 [8, 1], P('dp'), may hold values from 0 to 3
- family_tokens: int32 [4], replicated, may hold values from 100000 to 3999999
- norm_master: float32 [2048, 6], P('dp'), may hold values from -0.5 to 2.4, as said below
- attn_bias_master: float32 [2, 2048], P(None, 'mp'), may hold values from -2 to 2
- qkv_master: float32 [2048, 3, 2048], P('dp', None, 'mp'), may hold values from -0.125 to 0.125
- proj_master: float32 [2048, 2048], P('dp', 'mp'), may hold values from -1.5 to 1.5
- fc_bias_master: float32 [8192], P('mp'), may hold values from -1.5 to 1.5
- fc_master: float32 [2048, 8192], P('dp', 'mp'), may hold values from -0.125 to 0.125
- down_master: float32 [2048, 8192], P('dp', 'mp'), may hold values from -0.0625 to 0.0625
- norm_moment: float32 [2048, 6], P('dp'), may hold values from -0.0008544922 to 0.0008544922
- attn_bias_moment: float32 [2, 2048], P(None, 'mp'), may hold values from -0.0008544922 to 0.0008544922
- qkv_moment: float32 [2048, 3, 2048], P('dp', None, 'mp'), may hold values from -0.0008544922 to 0.0008544922
- proj_moment: float32 [2048, 2048], P('dp', 'mp'), may hold values from -0.0008544922 to 0.0008544922
- fc_bias_moment: float32 [8192], P('mp'), may hold values from -0.0008544922 to 0.0008544922
- fc_moment: float32 [2048, 8192], P('dp', 'mp'), may hold values from -0.0008544922 to 0.0008544922
- down_moment: float32 [2048, 8192], P('dp', 'mp'), may hold values from -0.0008544922 to 0.0008544922
- norm_average: float32 [2048, 6], P('dp'), may hold values from 0.5 to 1.5
- attn_bias_average: float32 [2, 2048], P(None, 'mp'), may hold values from -2 to 2
- qkv_average: float32 [2048, 3, 2048], P('dp', None, 'mp'), may hold values from -0.125 to 0.125
- proj_average: float32 [2048, 2048], P('dp', 'mp'), may hold values from -1.5 to 1.5
- fc_bias_average: float32 [8192], P('mp'), may hold values from -1.5 to 1.5
- fc_average: float32 [2048, 8192], P('dp', 'mp'), may hold values from -0.125 to 0.125
- down_average: float32 [2048, 8192], P('dp', 'mp'), may hold values from -0.0625 to 0.0625
Outputs:
- block_out: bfloat16 [8192, 2048], P('dp')
- input_grad: float32 [8192, 2048], P('dp')
- norm_grad: float32 [2048, 6], P('dp')
- attn_bias_grad: float32 [2, 2048], P(None, 'mp')
- qkv_grad: float32 [2048, 3, 2048], P('dp', None, 'mp')
- proj_grad: float32 [2048, 2048], P('dp', 'mp')
- fc_bias_grad: float32 [8192], P('mp')
- fc_grad: float32 [2048, 8192], P('dp', 'mp')
- down_grad: float32 [2048, 8192], P('dp', 'mp')
- norm_momentum: float32 [2048, 6], P('dp')
- attn_bias_momentum: float32 [2, 2048], P(None, 'mp')
- qkv_momentum: float32 [2048, 3, 2048], P('dp', None, 'mp')
- proj_momentum: float32 [2048, 2048], P('dp', 'mp')
- fc_bias_momentum: float32 [8192], P('mp')
- fc_momentum: float32 [2048, 8192], P('dp', 'mp')
- down_momentum: float32 [2048, 8192], P('dp', 'mp')
- norm_averaged: float32 [2048, 6], P('dp')
- attn_bias_averaged: float32 [2, 2048], P(None, 'mp')
- qkv_averaged: float32 [2048, 3, 2048], P('dp', None, 'mp')
- proj_averaged: float32 [2048, 2048], P('dp', 'mp')
- fc_bias_averaged: float32 [8192], P('mp')
- fc_averaged: float32 [2048, 8192], P('dp', 'mp')
- down_averaged: float32 [2048, 8192], P('dp', 'mp')
- norm_updated: float32 [2048, 6], P('dp')
- attn_bias_updated: float32 [2, 2048], P(None, 'mp')
- qkv_updated: float32 [2048, 3, 2048], P('dp', None, 'mp')
- proj_updated: float32 [2048, 2048], P('dp', 'mp')
- fc_bias_updated: float32 [8192], P('mp')
- fc_updated: float32 [2048, 8192], P('dp', 'mp')
- down_updated: float32 [2048, 8192], P('dp', 'mp')
- norm_copy: bfloat16 [2048, 6], P('dp')
- attn_bias_copy: bfloat16 [2, 2048], P(None, 'mp')
- qkv_copy: bfloat16 [2048, 3, 2048], P('dp', None, 'mp')
- proj_copy: bfloat16 [2048, 2048], P('dp', 'mp')
- fc_bias_copy: bfloat16 [8192], P('mp')
- fc_copy: bfloat16 [2048, 8192], P('dp', 'mp')
- down_copy: bfloat16 [2048, 8192], P('dp', 'mp')
- grad_norm: float32 [], replicated
Inputs may be any that keep to these rules, and one draw needn't show every extreme that they name: `lengths`: they sum to 6144; the longest is 1024. `seq_family`: every family has a sequence. `norm_master`: gains positive, biases of either sign.
All inputs are finite; a program needn't handle non-finite values. No bound on the sum of `lengths` on one device may be relied on, other than what follows from the above.
Results may differ from a plain program's by a relative error of at most 0.012.
The roundings to bfloat16 on the way count: a program that leaves them out, or rounds other values in their place, can miss the bound.
Values may be sent and summed in bfloat16 or wider, within the bound.
A program may use at most 256 MiB of HBM per device.

v0:
```python
import math
import jax
import jax.numpy as jnp
from jax import lax
from jax.sharding import PartitionSpec as P

HEAD_DIM = 128
LEN = 1024
EPS = 1e-05
MOMENTUM = 0.9
RATE = 192.0
KEEP = 0.9
NEG = -1e30


def layer_norm(value, gain, shift):
    centre = jnp.mean(value, axis=-1, keepdims=True)
    centred = value - centre
    spread = jnp.mean(centred * centred, axis=-1, keepdims=True)
    return centred * lax.rsqrt(spread + EPS) * gain + shift


def gelu_tanh(value):
    return (
        0.5
        * value
        * (1.0 + jnp.tanh(0.7978845608028654 * (value + 0.044715 * value * value * value)))
    )


def local(
    tokens,
    out_cot,
    lengths,
    seq_family,
    family_tokens,
    norm_master,
    attn_bias_master,
    qkv_master,
    proj_master,
    fc_bias_master,
    fc_master,
    down_master,
    norm_moment,
    attn_bias_moment,
    qkv_moment,
    proj_moment,
    fc_bias_moment,
    fc_moment,
    down_moment,
    norm_average,
    attn_bias_average,
    qkv_average,
    proj_average,
    fc_bias_average,
    fc_average,
    down_average,
):
    seq_count = lengths.shape[0]
    row_count = tokens.shape[0]
    seq_len = row_count // seq_count
    family_count = family_tokens.shape[0]
    local_heads = qkv_master.shape[2] // HEAD_DIM
    head_width = qkv_master.shape[2]
    scale = 1.0 / math.sqrt(HEAD_DIM)
    mp_count = lax.axis_size("mp")
    dp_count = lax.axis_size("dp")

    def sum_over_mp(term_fn):
        summed = lax.psum(term_fn(0, row_count), "mp")
        return summed

    family_ids = jnp.arange(family_count, dtype=jnp.int32)
    member = seq_family == family_ids[None, :]
    local_counts = jnp.sum(jnp.where(member, lengths[:, None], 0), axis=0).astype(jnp.float32)
    counts = lax.psum(local_counts, "dp")
    valid_total = jnp.sum(counts)
    share = family_tokens.astype(jnp.float32) / jnp.sum(family_tokens).astype(jnp.float32)
    family_weight = share * valid_total / jnp.maximum(counts, float(LEN // 2))
    seq_weight = jnp.sum(jnp.where(member, family_weight[None, :], 0.0), axis=1)
    places = jnp.arange(seq_len, dtype=jnp.int32)
    token_weight = jnp.where(places[None, :] < lengths[:, None], seq_weight[:, None], 0.0).reshape(
        row_count
    )
    causal = places[:, None] >= places[None, :]
    low_norm = norm_master.astype(jnp.bfloat16)
    low_qkv = qkv_master.astype(jnp.bfloat16)
    low_proj = proj_master.astype(jnp.bfloat16)
    low_fc = fc_master.astype(jnp.bfloat16)
    low_down = down_master.astype(jnp.bfloat16)
    w_qkv, w_proj, w_fc, w_down, w_norm = (
        lax.all_gather(low_qkv, "dp", axis=0, tiled=True),
        lax.all_gather(low_proj, "dp", axis=0, tiled=True),
        lax.all_gather(low_fc, "dp", axis=0, tiled=True),
        lax.all_gather(low_down, "dp", axis=0, tiled=True),
        lax.all_gather(low_norm, "dp", axis=0, tiled=True),
    )
    norm_full = w_norm.astype(jnp.float32)
    bias_rows = jnp.stack(
        [attn_bias_master[0], jnp.zeros_like(attn_bias_master[0]), attn_bias_master[1]], axis=0
    )
    x_in = tokens.astype(jnp.float32)
    ln1_low = layer_norm(x_in, norm_full[:, 0], norm_full[:, 1]).astype(jnp.bfloat16)
    qkv = (
        jnp.einsum("td,dce->tce", ln1_low, w_qkv, preferred_element_type=jnp.float32)
        + bias_rows[None]
    )
    qkv = qkv.astype(jnp.bfloat16)
    heads = qkv.reshape(seq_count, seq_len, 3, local_heads, HEAD_DIM)

    def attend(one_seq):
        query_rows = one_seq[:, 0]
        key_rows = one_seq[:, 1]
        value_rows = one_seq[:, 2]
        scores = (
            jnp.einsum("qhd,khd->hqk", query_rows, key_rows, preferred_element_type=jnp.float32)
            * scale
        )
        scores = jnp.where(causal[None], scores, NEG)
        row_top = jnp.max(scores, axis=-1, keepdims=True)
        log_total = row_top + jnp.log(jnp.sum(jnp.exp(scores - row_top), axis=-1, keepdims=True))
        attn_prob = jnp.exp(scores - log_total).astype(jnp.bfloat16)
        mixed = jnp.einsum(
            "hqk,khd->qhd", attn_prob, value_rows, preferred_element_type=jnp.float32
        )
        return (mixed.astype(jnp.bfloat16), log_total)

    mixed_low, log_kept = lax.map(attend, heads)
    mixed_low = mixed_low.reshape(row_count, head_width)

    def attn_term(start, count):
        return jnp.einsum("te,de->td", mixed_low, w_proj, preferred_element_type=jnp.float32)

    residual_part = x_in + sum_over_mp(attn_term) + norm_full[:, 4]
    ln2_part, ln2_back = jax.vjp(layer_norm, residual_part, norm_full[:, 2], norm_full[:, 3])
    ln2_low = ln2_part.astype(jnp.bfloat16)
    pre_act = (
        jnp.einsum("td,df->tf", ln2_low, w_fc, preferred_element_type=jnp.float32)
        + fc_bias_master[None]
    )
    hidden_act, gelu_back = jax.vjp(gelu_tanh, pre_act)
    hidden_low = hidden_act.astype(jnp.bfloat16)

    def mlp_term(start, count):
        return jnp.einsum("tf,df->td", hidden_low, w_down, preferred_element_type=jnp.float32)

    block_part = (residual_part + sum_over_mp(mlp_term) + norm_full[:, 5]).astype(jnp.bfloat16)
    upstream = token_weight[:, None] * out_cot.astype(jnp.float32)
    upstream_low = upstream.astype(jnp.bfloat16)
    down_sum = jnp.einsum("td,tf->df", upstream_low, hidden_low, preferred_element_type=jnp.float32)
    back_act = jnp.einsum("td,df->tf", upstream_low, w_down, preferred_element_type=jnp.float32)
    back_pre = gelu_back(back_act)[0].astype(jnp.bfloat16)
    fc_bias_sum = jnp.sum(back_pre, axis=0, dtype=jnp.float32)
    fc_sum = jnp.einsum("td,tf->df", ln2_low, back_pre, preferred_element_type=jnp.float32)

    def fc_back_term(start, count):
        return jnp.einsum("tf,df->td", back_pre, w_fc, preferred_element_type=jnp.float32)

    back_ln2 = sum_over_mp(fc_back_term)
    back_resid_part, gain2_sum, shift2_sum = ln2_back(back_ln2)
    back_resid_part = upstream + back_resid_part
    back_attn_low = back_resid_part.astype(jnp.bfloat16)
    proj_sum = jnp.einsum("td,te->de", back_attn_low, mixed_low, preferred_element_type=jnp.float32)
    back_mixed = jnp.einsum(
        "td,de->te", back_attn_low, w_proj, preferred_element_type=jnp.float32
    ).astype(jnp.bfloat16)
    back_mixed = back_mixed.reshape(seq_count, seq_len, local_heads, HEAD_DIM)

    def attend_back(items):
        one_seq, log_total, back_seq = items
        query_rows = one_seq[:, 0]
        key_rows = one_seq[:, 1]
        value_rows = one_seq[:, 2]
        scores = (
            jnp.einsum("qhd,khd->hqk", query_rows, key_rows, preferred_element_type=jnp.float32)
            * scale
        )
        scores = jnp.where(causal[None], scores, NEG)
        attn_prob = jnp.exp(scores - log_total)
        prob_low = attn_prob.astype(jnp.bfloat16)
        back_value = jnp.einsum(
            "hqk,qhd->khd", prob_low, back_seq, preferred_element_type=jnp.float32
        )
        back_prob = jnp.einsum(
            "qhd,khd->hqk", back_seq, value_rows, preferred_element_type=jnp.float32
        )
        back_score = attn_prob * (
            back_prob - jnp.sum(attn_prob * back_prob, axis=-1, keepdims=True)
        )
        back_score = back_score.astype(jnp.bfloat16)
        back_query = (
            jnp.einsum("hqk,khd->qhd", back_score, key_rows, preferred_element_type=jnp.float32)
            * scale
        )
        back_key = (
            jnp.einsum("hqk,qhd->khd", back_score, query_rows, preferred_element_type=jnp.float32)
            * scale
        )
        return jnp.stack([back_query, back_key, back_value], axis=1).astype(jnp.bfloat16)

    back_heads = lax.map(attend_back, (heads, log_kept, back_mixed))
    back_qkv = back_heads.reshape(row_count, 3, head_width)
    attn_bias_sum = jnp.sum(back_qkv[:, 0::2], axis=0, dtype=jnp.float32)
    qkv_sum = jnp.einsum("td,tce->dce", ln1_low, back_qkv, preferred_element_type=jnp.float32)

    def qkv_back_term(start, count):
        return jnp.einsum("tce,dce->td", back_qkv, w_qkv, preferred_element_type=jnp.float32)

    back_ln1 = sum_over_mp(qkv_back_term)
    ln1_again, ln1_back = jax.vjp(layer_norm, x_in, norm_full[:, 0], norm_full[:, 1])
    back_input, gain1_sum, shift1_sum = ln1_back(back_ln1)
    whole = back_resid_part + back_input
    norm_part = jnp.stack(
        [
            gain1_sum,
            shift1_sum,
            gain2_sum,
            shift2_sum,
            jnp.sum(back_resid_part, axis=0),
            jnp.sum(upstream, axis=0),
        ],
        axis=1,
    )
    qkv_reduced, proj_reduced, fc_reduced, down_reduced, norm_reduced = (
        lax.psum_scatter(qkv_sum, "dp", scatter_dimension=0, tiled=True),
        lax.psum_scatter(proj_sum, "dp", scatter_dimension=0, tiled=True),
        lax.psum_scatter(fc_sum, "dp", scatter_dimension=0, tiled=True),
        lax.psum_scatter(down_sum, "dp", scatter_dimension=0, tiled=True),
        lax.psum_scatter(norm_part, "dp", scatter_dimension=0, tiled=True),
    )
    attn_bias_reduced, fc_bias_reduced = lax.psum((attn_bias_sum, fc_bias_sum), "dp")
    raw_grads = [
        reduced / valid_total
        for reduced in (
            norm_reduced,
            attn_bias_reduced,
            qkv_reduced,
            proj_reduced,
            fc_bias_reduced,
            fc_reduced,
            down_reduced,
        )
    ]
    local_squares = jnp.sum(raw_grads[0] * raw_grads[0]) / float(mp_count)
    local_squares = local_squares + jnp.sum(raw_grads[1] * raw_grads[1]) / float(dp_count)
    local_squares = local_squares + jnp.sum(raw_grads[4] * raw_grads[4]) / float(dp_count)
    for grad_raw in (raw_grads[2], raw_grads[3], raw_grads[5], raw_grads[6]):
        local_squares = local_squares + jnp.sum(grad_raw * grad_raw)
    squares = lax.psum(local_squares, ("dp", "mp"))
    grad_norm = jnp.sqrt(squares)
    clip_factor = jnp.minimum(1.0, 1.0 / (grad_norm + 1e-06))
    masters = (
        norm_master,
        attn_bias_master,
        qkv_master,
        proj_master,
        fc_bias_master,
        fc_master,
        down_master,
    )
    moments = (
        norm_moment,
        attn_bias_moment,
        qkv_moment,
        proj_moment,
        fc_bias_moment,
        fc_moment,
        down_moment,
    )
    averages = (
        norm_average,
        attn_bias_average,
        qkv_average,
        proj_average,
        fc_bias_average,
        fc_average,
        down_average,
    )
    grads_out = []
    momenta_out = []
    averaged_out = []
    updated_out = []
    copies_out = []
    for master, moment, average, grad_raw in zip(masters, moments, averages, raw_grads):
        clipped = grad_raw * clip_factor
        momentum = MOMENTUM * moment + clipped
        updated = master - RATE * (clipped + MOMENTUM * momentum)
        averaged = KEEP * average + (1.0 - KEEP) * updated
        grads_out.append(clipped)
        momenta_out.append(momentum)
        averaged_out.append(averaged)
        updated_out.append(updated)
        copies_out.append(updated.astype(jnp.bfloat16))
    return (
        block_part,
        whole,
        grads_out[0],
        grads_out[1],
        grads_out[2],
        grads_out[3],
        grads_out[4],
        grads_out[5],
        grads_out[6],
        momenta_out[0],
        momenta_out[1],
        momenta_out[2],
        momenta_out[3],
        momenta_out[4],
        momenta_out[5],
        momenta_out[6],
        averaged_out[0],
        averaged_out[1],
        averaged_out[2],
        averaged_out[3],
        averaged_out[4],
        averaged_out[5],
        averaged_out[6],
        updated_out[0],
        updated_out[1],
        updated_out[2],
        updated_out[3],
        updated_out[4],
        updated_out[5],
        updated_out[6],
        copies_out[0],
        copies_out[1],
        copies_out[2],
        copies_out[3],
        copies_out[4],
        copies_out[5],
        copies_out[6],
        grad_norm,
    )


def solution(mesh):
    placed = (
        P("dp", None),
        P("dp", None),
        P("dp"),
        P("dp", None),
        P(),
        P("dp", None),
        P(None, "mp"),
        P("dp", None, "mp"),
        P("dp", "mp"),
        P("mp"),
        P("dp", "mp"),
        P("dp", "mp"),
        P("dp", None),
        P(None, "mp"),
        P("dp", None, "mp"),
        P("dp", "mp"),
        P("mp"),
        P("dp", "mp"),
        P("dp", "mp"),
        P("dp", None),
        P(None, "mp"),
        P("dp", None, "mp"),
        P("dp", "mp"),
        P("mp"),
        P("dp", "mp"),
        P("dp", "mp"),
    )
    return jax.shard_map(
        local,
        mesh=mesh,
        in_specs=placed,
        out_specs=(
            P("dp", None),
            P("dp", None),
            P("dp", None),
            P(None, "mp"),
            P("dp", None, "mp"),
            P("dp", "mp"),
            P("mp"),
            P("dp", "mp"),
            P("dp", "mp"),
            P("dp", None),
            P(None, "mp"),
            P("dp", None, "mp"),
            P("dp", "mp"),
            P("mp"),
            P("dp", "mp"),
            P("dp", "mp"),
            P("dp", None),
            P(None, "mp"),
            P("dp", None, "mp"),
            P("dp", "mp"),
            P("mp"),
            P("dp", "mp"),
            P("dp", "mp"),
            P("dp", None),
            P(None, "mp"),
            P("dp", None, "mp"),
            P("dp", "mp"),
            P("mp"),
            P("dp", "mp"),
            P("dp", "mp"),
            P("dp", None),
            P(None, "mp"),
            P("dp", None, "mp"),
            P("dp", "mp"),
            P("mp"),
            P("dp", "mp"),
            P("dp", "mp"),
            P(),
        ),
        check_vma=False,
    )
```

profile of v0, /device:TPU:0, one launch (start us, length us, event | category | flops | bytes accessed | tf_op | source)
XLA Modules:
  0.0 2152.3 jit_solution(12280135592228971859)
XLA Ops:
  19.1 32.9 %all_gather.15 = bf16[2048,6]{0,1:T(8,128)(2,1)S(1)} all-gather(bf16[256,6]{0,1:T(8,128)(2,1)S(1)} %convert_element_type.108), channel_id=1, replica_groups=mesh['dp'=8,'mp'=4] {'dp'}, dimensions={0}, use_global_device_ids=true | all-gather | bytes 27648 | tf_op jit(solution)/shard_map/all_gather | solution.py:96
  52.7 61.0 %all-gather.5.cloned.1.call-done = bf16[2048,3,512]{0,2,1:T(8,128)(2,1)} async-done(((bf16[256,3,512]{0,2,1:T(8,128)(2,1)}), bf16[2048,3,512]{0,2,1:T(8,128)(2,1)}) %all-gather.5.cloned.1.call-update) | async-done | bytes 6291472 | tf_op jit(solution)/shard_map/all_gather | solution.py:92
  113.7 11.1 add_convert_fusion.2
  140.5 23.5 %all-gather.7.cloned.1.call-done = bf16[2048,512]{1,0:T(8,128)(2,1)} async-done(((bf16[256,512]{1,0:T(8,128)(2,1)}), bf16[2048,512]{1,0:T(8,128)(2,1)}) %all-gather.7.cloned.1.call-update) | async-done | bytes 2097168 | tf_op jit(solution)/shard_map/all_gather | solution.py:93
  178.8 18.5 psum.58
  201.1 121.8 %all-reduce.6.cloned.1.call-done = f32[1024,2048]{1,0:T(8,128)} async-done(((f32[1024,2048]{1,0:T(8,128)}), f32[1024,2048]{1,0:T(8,128)}) %all-reduce.6.cloned.1.call-update) | async-done | bytes 8388624 | tf_op jit(solution)/shard_map/psum | solution.py:70
  333.0 117.6 %all-gather.9.cloned.1.call-done = bf16[2048,2048]{1,0:T(8,128)(2,1)} async-done(((bf16[256,2048]{1,0:T(8,128)(2,1)}), bf16[2048,2048]{1,0:T(8,128)(2,1)}) %all-gather.9.cloned.1.call-update) | async-done | bytes 8388624 | tf_op jit(solution)/shard_map/all_gather | solution.py:94
  450.6 15.9 fusion.51
  466.5 109.8 %all-gather.11.cloned.1.call-done = bf16[2048,2048]{1,0:T(8,128)(2,1)} async-done(((bf16[256,2048]{1,0:T(8,128)(2,1)}), bf16[2048,2048]{1,0:T(8,128)(2,1)}) %all-gather.11.cloned.1.call-update) | async-done | bytes 8388624 | tf_op jit(solution)/shard_map/all_gather | solution.py:95
  576.3 21.0 convert_reduce_fusion.1
  610.3 18.3 fusion.49
  628.6 132.9 %all-reduce.8.cloned.1.call-done = f32[1024,2048]{1,0:T(8,128)} async-done(((f32[1024,2048]{1,0:T(8,128)}), f32[1024,2048]{1,0:T(8,128)}) %all-reduce.8.cloned.1.call-update) | async-done | bytes 8388624 | tf_op jit(solution)/shard_map/psum | solution.py:70
  790.7 12.6 multiply_reduce_fusion
  803.3 12.1 multiply_convert_fusion
  844.9 278.3 %all-reduce.10.cloned.1.call-done = (f32[1024,2048]{1,0:T(8,128)}, f32[1024,2048]{1,0:T(8,128)}) async-done(((f32[1024,2048]{1,0:T(8,128)}, f32[1024,2048]{1,0:T(8,128)}), (f32[1024,2048]{1,0:T(8,128)}, f32[1024,2048]{1,0:T(8,128)})) %all-reduce.10.cloned.1.call-update) | async-done | bytes 16777232 | tf_op jit(solution)/shard_map/psum | solution.py:70
  1146.7 13.6 fusion.36
  1161.0 16.4 fusion.50
  1177.7 17.1 fusion.27
  1195.5 37.8 %all-reduce = (f32[2,512]{1,0:T(2,128)S(1)}, f32[2048]{0:T(1024)S(1)}) all-reduce(f32[2,512]{1,0:T(2,128)S(1)} %convert_reduce_fusion.2, f32[2048]{0:T(1024)S(1)} %copy-done.48), channel_id=1, replica_groups=mesh['dp'=8,'mp'=4] {'dp'}, use_global_device_ids=true, to_apply=%region_28.29 | all-reduce | flops 3072 | bytes 24576 | tf_op jit(solution)/shard_map/psum | solution.py:231
  1239.6 41.7 %reduce-scatter.6.cloned.1.call-done = f32[256,6]{0,1:T(8,128)} async-done(((f32[2048,6]{0,1:T(8,128)}), f32[256,6]{0,1:T(8,128)}) %reduce-scatter.6.cloned.1.call-update) | async-done | bytes 6160 | tf_op jit(solution)/shard_map/reduce_scatter | solution.py:229
  1283.9 208.1 %reduce-scatter.8.cloned.1.call-done = f32[256,3,512]{2,0,1:T(8,128)} async-done(((f32[2048,3,512]{2,0,1:T(8,128)}), f32[256,3,512]{2,0,1:T(8,128)}) %reduce-scatter.8.cloned.1.call-update) | async-done | bytes 1572880 | tf_op jit(solution)/shard_map/reduce_scatter | solution.py:225
  1496.3 280.9 %reduce-scatter.12.cloned.1.call-done = f32[256,2048]{1,0:T(8,128)} async-done(((f32[2048,2048]{1,0:T(8,128)}), f32[256,2048]{1,0:T(8,128)}) %reduce-scatter.12.cloned.1.call-update) | async-done | bytes 2097168 | tf_op jit(solution)/shard_map/reduce_scatter | solution.py:227
  1781.3 281.4 %reduce-scatter.14.cloned.1.call-done = f32[256,2048]{1,0:T(8,128)} async-done(((f32[2048,2048]{1,0:T(8,128)}), f32[256,2048]{1,0:T(8,128)}) %reduce-scatter.14.cloned.1.call-update) | async-done | bytes 2097168 | tf_op jit(solution)/shard_map/reduce_scatter | solution.py:228
  2077.0 39.2 %psum.63 = f32[]{:T(128)} all-reduce(f32[]{:T(128)S(6)} %add.249), channel_id=1, replica_groups=mesh['dp'=8,'mp'=4] {'dp','mp'}, use_global_device_ids=true, to_apply=%region_41.42 | all-reduce | flops 1 | bytes 8 | tf_op jit(solution)/shard_map/psum | solution.py:249
  (214 shorter events, 205.2 us)
Async XLA Ops:
  7.2 106.5 %all-gather.5.cloned.1.call-start = ((), (), s32[]{:S(2)}) async-start(), calls=%async_computation.5 | async-start | bytes 7077888 | tf_op jit(solution)/shard_map/all_gather | solution.py:92
  9.9 154.1 %all-gather.7.cloned.1.call-start = ((), (), s32[]{:S(2)}) async-start(), calls=%async_computation.6 | async-start | bytes 2359296 | tf_op jit(solution)/shard_map/all_gather | solution.py:93
  11.7 311.2 %all-reduce.6.cloned.1.call-start = ((), (), s32[]{:S(2)}) async-start(), calls=%async_computation.7 | async-start | bytes 16777216 | tf_op jit(solution)/shard_map/psum | solution.py:70
  15.6 109.2 %copy-start.28 = (f32[1024]{0:T(1024)}, f32[1024]{0:T(1024)S(1)}, u32[]{:S(2)}) copy-start(f32[1024]{0:T(1024)S(1)} %broadcast_multiply_fusion.8) | copy-start | bytes 12292
  19.0 105.8 %copy-start.32 = (f32[1024]{0:T(1024)}, f32[1024]{0:T(1024)S(1)}, u32[]{:S(2)}) copy-start(f32[1024]{0:T(1024)S(1)} %fusion.15) | copy-start | bytes 12292
  19.1 105.8 %copy-start.30 = (f32[1024]{0:T(1024)}, f32[1024]{0:T(1024)S(1)}, u32[]{:S(2)}) copy-start(f32[1024]{0:T(1024)S(1)} %fusion.42) | copy-start | bytes 12292
  52.6 72.3 %copy-start.26 = (f32[2048,1]{0,1:T(1,128)}, f32[2048,1]{0,1:T(1,128)S(1)}, u32[]{:S(2)}) copy-start(f32[2048,1]{0,1:T(1,128)S(1)} %get-tuple-element.123) | copy-start | bytes 24580
  52.6 72.3 %copy-start.46 = (f32[2048,1]{0,1:T(1,128)}, f32[2048,1]{0,1:T(1,128)S(1)}, u32[]{:S(2)}) copy-start(f32[2048,1]{0,1:T(1,128)S(1)} %get-tuple-element.124) | copy-start | bytes 24580
  52.6 398.0 %copy-start.44 = (f32[2048,1]{0,1:T(1,128)}, f32[2048,1]{0,1:T(1,128)S(1)}, u32[]{:S(2)}) copy-start(f32[2048,1]{0,1:T(1,128)S(1)} %get-tuple-element.121) | copy-start | bytes 24580
  171.4 279.2 %all-gather.9.cloned.1.call-start = ((), (), s32[]{:S(2)}) async-start(), calls=%async_computation.8 | async-start | bytes 9437184 | tf_op jit(solution)/shard_map/all_gather | solution.py:94
  174.2 402.1 %all-gather.11.cloned.1.call-start = ((), (), s32[]{:S(2)}) async-start(), calls=%async_computation.9 | async-start | bytes 9437184 | tf_op jit(solution)/shard_map/all_gather | solution.py:95
  177.5 584.0 %all-reduce.8.cloned.1.call-start = ((), (), s32[]{:S(2)}) async-start(), calls=%async_computation.10 | async-start | bytes 16777216 | tf_op jit(solution)/shard_map/psum | solution.py:70
  450.6 125.7 %copy-start.49 = (f32[2048]{0:T(1024)S(1)}, f32[2048]{0:T(1024)}, u32[]{:S(2)}) copy-start(f32[2048]{0:T(1024)} %param.35) | copy-start | bytes 24580
  610.3 513.0 %all-reduce.10.cloned.1.call-start = ((), (), s32[]{:S(2)}) async-start(), calls=%async_computation.16 | async-start | bytes 33554432 | tf_op jit(solution)/shard_map/psum | solution.py:70
  834.1 289.2 %copy-start.27 = (f32[2048,1]{0,1:T(1,128)S(1)}, f32[2048,1]{0,1:T(1,128)}, u32[]{:S(2)}) copy-start(f32[2048,1]{0,1:T(1,128)} %copy-done.26) | copy-start | bytes 24580
  834.1 289.1 %copy-start.29 = (f32[1024]{0:T(1024)S(1)}, f32[1024]{0:T(1024)}, u32[]{:S(2)}) copy-start(f32[1024]{0:T(1024)} %copy-done.28) | copy-start | bytes 12292
  834.1 403.0 %reduce-scatter.10.cloned.1.call-start = ((), (), s32[]{:S(2)}) async-start(), calls=%async_computation.13 | async-start | bytes 4718592 | tf_op jit(solution)/shard_map/reduce_scatter | solution.py:226
  844.8 284.8 %copy-start.33 = (f32[1024]{0:T(1024)S(1)}, f32[1024]{0:T(1024)}, u32[]{:S(2)}) copy-start(f32[1024]{0:T(1024)} %copy-done.32) | copy-start | bytes 12292
  844.8 284.8 %copy-start.31 = (f32[1024]{0:T(1024)S(1)}, f32[1024]{0:T(1024)}, u32[]{:S(2)}) copy-start(f32[1024]{0:T(1024)} %copy-done.30) | copy-start | bytes 12292
  844.9 436.4 %reduce-scatter.6.cloned.1.call-start = ((), (), s32[]{:S(2)}) async-start(), calls=%async_computation.11 | async-start | bytes 73728 | tf_op jit(solution)/shard_map/reduce_scatter | solution.py:229
  1146.5 345.5 %reduce-scatter.8.cloned.1.call-start = ((), (), s32[]{:S(2)}) async-start(), calls=%async_computation.12 | async-start | bytes 14155776 | tf_op jit(solution)/shard_map/reduce_scatter | solution.py:225
  1160.3 616.9 %reduce-scatter.12.cloned.1.call-start = ((), (), s32[]{:S(2)}) async-start(), calls=%async_computation.14 | async-start | bytes 18874368 | tf_op jit(solution)/shard_map/reduce_scatter | solution.py:227
  1177.4 885.3 %reduce-scatter.14.cloned.1.call-start = ((), (), s32[]{:S(2)}) async-start(), calls=%async_computation.15 | async-start | bytes 18874368 | tf_op jit(solution)/shard_map/reduce_scatter | solution.py:228
  1194.8 871.9 %copy-start.34 = (f32[2048,1]{0,1:T(1,128)S(1)}, f32[2048,1]{0,1:T(1,128)}, u32[]{:S(2)}) copy-start(f32[2048,1]{0,1:T(1,128)} %get-tuple-element.119) | copy-start | bytes 24580
  (47 other events, 938.4 us)
Sparse Core Ops, SparseCore 0:
  10.7 102.9 all-gather.4
  116.4 47.5 all-gather.6
  171.5 151.3 all-reduce.5
  325.5 125.0 all-gather.8
  453.1 123.1 all-gather.10
  610.4 151.0 all-reduce.7
  834.2 288.9 all-reduce.9
  1127.5 88.2 reduce-scatter.9
  1220.1 61.1 reduce-scatter.5
  1285.1 206.7 reduce-scatter.7
  1496.2 280.9 reduce-scatter.11
  1780.9 281.7 reduce-scatter.13
where the time goes:
time: 2160 us; the launch traced here: 2150 us
  waiting for transfers between devices  1660 us (77%)
  matrix products  195 us (9%)
  other arithmetic  128 us (6%)
  blocking collectives  128 us (6%)
  between operations  23.6 us (1%)
    psum x3, waiting for transfers between devices, sum_over_mp(): summed = lax.psum(term_fn(0, row_count), 'mp')  533 us
    reduce_scatter x1, waiting for transfers between devices, local(): lax.psum_scatter(down_sum, 'dp', scatter_dimension=0, tiled=True)  281 us
    reduce_scatter x1, waiting for transfers between devices, local(): lax.psum_scatter(fc_sum, 'dp', scatter_dimension=0, tiled=True)  281 us
    reduce_scatter x1, waiting for transfers between devices, local(): lax.psum_scatter(qkv_sum, 'dp', scatter_dimension=0, tiled=True)  208 us
    all_gather x1, waiting for transfers between devices, local(): lax.all_gather(low_fc, 'dp', axis=0, tiled=True)  118 us
    all_gather x1, waiting for transfers between devices, local(): lax.all_gather(low_down, 'dp', axis=0, tiled=True)  110 us
    all_gather x1, waiting for transfers between devices, local(): lax.all_gather(low_qkv, 'dp', axis=0, tiled=True)  61 us
  transfers between devices with their start and end apart: 12, of which 11 were waited for; matrix products, arithmetic and copies ran while one was open for 8% of the time, Pallas kernels for 0%

commit v1 on v0

--- a/solution.py
+++ b/solution.py
@@ -11,6 +11,18 @@
 RATE = 192.0
 KEEP = 0.9
 NEG = -1e30
+
+
+def collect(x, axis, dim):
+    ways, here = (lax.axis_size(axis), lax.axis_index(axis))
+    grown, reach = (x, 1)
+    while reach < ways:
+        theirs = lax.ppermute(grown, axis, [(d, d ^ reach) for d in range(ways)])
+        mine_first = jnp.concatenate([grown, theirs], axis=dim)
+        theirs_first = jnp.concatenate([theirs, grown], axis=dim)
+        grown = jnp.where(here & reach == 0, mine_first, theirs_first)
+        reach = 2 * reach
+    return grown
 
 
 def layer_norm(value, gain, shift):
@@ -91,7 +103,7 @@
     w_qkv, w_proj, w_fc, w_down, w_norm = (
         lax.all_gather(low_qkv, "dp", axis=0, tiled=True),
         lax.all_gather(low_proj, "dp", axis=0, tiled=True),
-        lax.all_gather(low_fc, "dp", axis=0, tiled=True),
+        collect(low_fc, "dp", 0),
         lax.all_gather(low_down, "dp", axis=0, tiled=True),
         lax.all_gather(low_norm, "dp", axis=0, tiled=True),
     )

time: 2160 us -> 2170 us (level)
  waiting for transfers between devices: 1660 us -> 1550 us
  blocking collectives: 128 us -> 226 us
    ppermute x0 -> x3, waiting for transfers between devices: none -> 216 us  [collect(): theirs = lax.ppermute(grown, axis, [(d, d ^ reach) for d in range(ways)])]
    all_gather x1 -> x0, waiting for transfers between devices: 118 us -> none  [local(): lax.all_gather(low_fc, 'dp', axis=0, tiled=True)]
    all_gather x1, waiting for transfers between devices: 110 us -> 0.01 us  [local(): lax.all_gather(low_down, 'dp', axis=0, tiled=True)]
    psum x1, blocking collectives: 18.5 us -> 116 us  [local(): counts = lax.psum(local_counts, 'dp')]
    psum x3, waiting for transfers between devices: 533 us -> 436 us  [sum_over_mp(): summed = lax.psum(term_fn(0, row_count), 'mp')]
  transfers between devices with their start and end apart: 12 -> 14, of which waited for: 11 -> 11; matrix products, arithmetic and copies ran while one was open for 8% -> 9% of each run, Pallas kernels for 0% -> 0%
where the time goes in v1:
time: 2170 us; the launch traced here: 2160 us
  waiting for transfers between devices  1550 us (71%)
  blocking collectives  226 us (10%)
  matrix products  206 us (9%)
  other arithmetic  137 us (6%)
  between operations  23.3 us (1%)
    psum x3, waiting for transfers between devices, sum_over_mp(): summed = lax.psum(term_fn(0, row_count), 'mp')  436 us
    reduce_scatter x1, waiting for transfers between devices, local(): lax.psum_scatter(down_sum, 'dp', scatter_dimension=0, tiled=True)  281 us
    reduce_scatter x1, waiting for transfers between devices, local(): lax.psum_scatter(fc_sum, 'dp', scatter_dimension=0, tiled=True)  281 us
    ppermute x3, waiting for transfers between devices, collect(): theirs = lax.ppermute(grown, axis, [(d, d ^ reach) for d in range(ways)])  216 us
    reduce_scatter x1, waiting for transfers between devices, local(): lax.psum_scatter(qkv_sum, 'dp', scatter_dimension=0, tiled=True)  208 us
    psum x1, blocking collectives, local(): counts = lax.psum(local_counts, 'dp')  116 us
    all_gather x1, waiting for transfers between devices, local(): lax.all_gather(low_qkv, 'dp', axis=0, tiled=True)  61 us
  transfers between devices with their start and end apart: 14, of which 11 were waited for; matrix products, arithmetic and copies ran while one was open for 9% of the time, Pallas kernels for 0%

profile of v1, /device:TPU:0, one launch (start us, length us, event | category | flops | bytes accessed | tf_op | source)
XLA Modules:
  0.0 2164.3 jit_solution(18439398517802579553)
XLA Ops:
  19.1 32.9 %all_gather.12 = bf16[2048,6]{0,1:T(8,128)(2,1)S(1)} all-gather(bf16[256,6]{0,1:T(8,128)(2,1)S(1)} %convert_element_type.108), channel_id=1, replica_groups=mesh['dp'=8,'mp'=4] {'dp'}, dimensions={0}, use_global_device_ids=true | all-gather | bytes 27648 | tf_op jit(solution)/shard_map/all_gather | solution.py:108
  52.7 61.0 %all-gather.4.cloned.1.call-done = bf16[2048,3,512]{0,2,1:T(8,128)(2,1)} async-done(((bf16[256,3,512]{0,2,1:T(8,128)(2,1)}), bf16[2048,3,512]{0,2,1:T(8,128)(2,1)}) %all-gather.4.cloned.1.call-update) | async-done | bytes 6291472 | tf_op jit(solution)/shard_map/all_gather | solution.py:104
  140.4 23.5 %all-gather.6.cloned.1.call-done = bf16[2048,512]{1,0:T(8,128)(2,1)} async-done(((bf16[256,512]{1,0:T(8,128)(2,1)}), bf16[2048,512]{1,0:T(8,128)(2,1)}) %all-gather.6.cloned.1.call-update) | async-done | bytes 2097168 | tf_op jit(solution)/shard_map/all_gather | solution.py:105
  176.6 23.3 %collective-permute-done = bf16[256,2048]{1,0:T(8,128)(2,1)} collective-permute-done((bf16[256,2048]{1,0:T(8,128)(2,1)S(1)}, bf16[256,2048]{1,0:T(8,128)(2,1)}, u32[]{:S(2)}, u32[]{:S(2)}) %collective-permute-start) | collective-permute-done | bytes 1048608 | tf_op jit(solution)/shard_map/ppermute | solution.py:20
  205.5 44.1 %collective-permute-done.1 = bf16[512,2048]{1,0:T(8,128)(2,1)} collective-permute-done((bf16[512,2048]{1,0:T(8,128)(2,1)}, bf16[512,2048]{1,0:T(8,128)(2,1)}, u32[]{:S(2)}, u32[]{:S(2)}) %collective-permute-start.1) | collective-permute-done | bytes 2097184 | tf_op jit(solution)/shard_map/ppermute | solution.py:20
  260.0 116.4 %psum.58 = f32[4]{0:T(128)S(1)} all-reduce(f32[4]{0:T(128)S(1)} %fusion.46), channel_id=1, replica_groups=mesh['dp'=8,'mp'=4] {'dp'}, use_global_device_ids=true, to_apply=%region_9.10 | all-reduce | flops 4 | bytes 32 | tf_op jit(solution)/shard_map/psum | solution.py:88
  390.3 148.6 %collective-permute-done.2 = bf16[1024,2048]{1,0:T(8,128)(2,1)} collective-permute-done((bf16[1024,2048]{1,0:T(8,128)(2,1)}, bf16[1024,2048]{1,0:T(8,128)(2,1)}, u32[]{:S(2)}, u32[]{:S(2)}) %collective-permute-start.2) | collective-permute-done | bytes 4194336 | tf_op jit(solution)/shard_map/ppermute | solution.py:20
  538.9 17.3 fusion.37
  556.2 23.0 %convert_reduce_fusion.1 = (f32[2048]{0:T(1024)}, bf16[1024,2048]{1,0:T(8,128)(2,1)}) fusion(bf16[2048,2048]{1,0:T(8,128)(2,1)} %all-gather.8.cloned.1.call-done, bf16[1024,2048]{1,0:T(8,128)(2,1)} %param.27, f32[1024]{0:T(1024)S(1)} %fusion.43, f32[1024,2048]{1,0:T(8,128)} %fusion.37, f32[2048]{0:T(1024)S(1)} %copy-done.49), kind=kOutput, calls=%fused_computation.35 | convolution fusion | flops 8652847104 | bytes 25186304 | tf_op jit(solution)/shard_map/td,df->tf/dot_general | solution.py:163
  579.2 19.3 fusion.36
  598.5 17.5 fusion.53
  616.0 157.7 %all-reduce.8.cloned.1.call-done = f32[1024,2048]{1,0:T(8,128)} async-done(((f32[1024,2048]{1,0:T(8,128)}), f32[1024,2048]{1,0:T(8,128)}) %all-reduce.8.cloned.1.call-update) | async-done | bytes 8388624 | tf_op jit(solution)/shard_map/psum | solution.py:82
  803.0 12.6 multiply_reduce_fusion
  815.6 12.1 multiply_convert_fusion
  857.2 278.3 %all-reduce.10.cloned.1.call-done = (f32[1024,2048]{1,0:T(8,128)}, f32[1024,2048]{1,0:T(8,128)}) async-done(((f32[1024,2048]{1,0:T(8,128)}, f32[1024,2048]{1,0:T(8,128)}), (f32[1024,2048]{1,0:T(8,128)}, f32[1024,2048]{1,0:T(8,128)})) %all-reduce.10.cloned.1.call-update) | async-done | bytes 16777232 | tf_op jit(solution)/shard_map/psum | solution.py:82
  1159.0 13.6 fusion.38
  1173.3 16.4 fusion.54
  1190.0 17.1 fusion.27
  1207.8 37.8 %all-reduce = (f32[2,512]{1,0:T(2,128)S(1)}, f32[2048]{0:T(1024)S(1)}) all-reduce(f32[2,512]{1,0:T(2,128)S(1)} %convert_reduce_fusion.2, f32[2048]{0:T(1024)S(1)} %copy-done.48), channel_id=1, replica_groups=mesh['dp'=8,'mp'=4] {'dp'}, use_global_device_ids=true, to_apply=%region_28.29 | all-reduce | flops 3072 | bytes 24576 | tf_op jit(solution)/shard_map/psum | solution.py:243
  1251.9 41.6 %reduce-scatter.6.cloned.1.call-done = f32[256,6]{0,1:T(8,128)} async-done(((f32[2048,6]{0,1:T(8,128)}), f32[256,6]{0,1:T(8,128)}) %reduce-scatter.6.cloned.1.call-update) | async-done | bytes 6160 | tf_op jit(solution)/shard_map/reduce_scatter | solution.py:241
  1296.1 208.2 %reduce-scatter.8.cloned.1.call-done = f32[256,3,512]{2,0,1:T(8,128)} async-done(((f32[2048,3,512]{2,0,1:T(8,128)}), f32[256,3,512]{2,0,1:T(8,128)}) %reduce-scatter.8.cloned.1.call-update) | async-done | bytes 1572880 | tf_op jit(solution)/shard_map/reduce_scatter | solution.py:237
  1508.7 280.9 %reduce-scatter.12.cloned.1.call-done = f32[256,2048]{1,0:T(8,128)} async-done(((f32[2048,2048]{1,0:T(8,128)}), f32[256,2048]{1,0:T(8,128)}) %reduce-scatter.12.cloned.1.call-update) | async-done | bytes 2097168 | tf_op jit(solution)/shard_map/reduce_scatter | solution.py:239
  1793.7 281.4 %reduce-scatter.14.cloned.1.call-done = f32[256,2048]{1,0:T(8,128)} async-done(((f32[2048,2048]{1,0:T(8,128)}), f32[256,2048]{1,0:T(8,128)}) %reduce-scatter.14.cloned.1.call-update) | async-done | bytes 2097168 | tf_op jit(solution)/shard_map/reduce_scatter | solution.py:240
  2089.4 39.1 %psum.63 = f32[]{:T(128)} all-reduce(f32[]{:T(128)S(6)} %add.249), channel_id=1, replica_groups=mesh['dp'=8,'mp'=4] {'dp','mp'}, use_global_device_ids=true, to_apply=%region_41.42 | all-reduce | flops 1 | bytes 8 | tf_op jit(solution)/shard_map/psum | solution.py:261
  (215 shorter events, 217.1 us)
Async XLA Ops:
  7.2 106.5 %all-gather.4.cloned.1.call-start = ((), (), s32[]{:S(2)}) async-start(), calls=%async_computation.5 | async-start | bytes 7077888 | tf_op jit(solution)/shard_map/all_gather | solution.py:104
  9.9 154.1 %all-gather.6.cloned.1.call-start = ((), (), s32[]{:S(2)}) async-start(), calls=%async_computation.6 | async-start | bytes 2359296 | tf_op jit(solution)/shard_map/all_gather | solution.py:105
  11.7 368.5 %all-reduce.6.cloned.1.call-start = ((), (), s32[]{:S(2)}) async-start(), calls=%async_computation.7 | async-start | bytes 16777216 | tf_op jit(solution)/shard_map/psum | solution.py:82
  15.6 109.2 %copy-start.28 = (f32[1024]{0:T(1024)}, f32[1024]{0:T(1024)S(1)}, u32[]{:S(2)}) copy-start(f32[1024]{0:T(1024)S(1)} %broadcast_multiply_fusion.8) | copy-start | bytes 12292
  19.0 105.8 %copy-start.32 = (f32[1024]{0:T(1024)}, f32[1024]{0:T(1024)S(1)}, u32[]{:S(2)}) copy-start(f32[1024]{0:T(1024)S(1)} %fusion.15) | copy-start | bytes 12292
  19.1 105.8 %copy-start.30 = (f32[1024]{0:T(1024)}, f32[1024]{0:T(1024)S(1)}, u32[]{:S(2)}) copy-start(f32[1024]{0:T(1024)S(1)} %fusion.44) | copy-start | bytes 12292
  52.6 486.3 %copy-start.44 = (f32[2048,1]{0,1:T(1,128)}, f32[2048,1]{0,1:T(1,128)S(1)}, u32[]{:S(2)}) copy-start(f32[2048,1]{0,1:T(1,128)S(1)} %get-tuple-element.121) | copy-start | bytes 24580
  171.4 384.8 %all-gather.8.cloned.1.call-start = ((), (), s32[]{:S(2)}) async-start(), calls=%async_computation.8 | async-start | bytes 9437184 | tf_op jit(solution)/shard_map/all_gather | solution.py:107
  174.2 202.2 %copy-start.54 = (s32[4]{0:T(128)S(1)}, s32[4]{0:T(128)}, u32[]{:S(2)}) copy-start(s32[4]{0:T(128)} %param.30) | copy-start | bytes 52
  174.2 599.5 %all-reduce.8.cloned.1.call-start = ((), (), s32[]{:S(2)}) async-start(), calls=%async_computation.9 | async-start | bytes 16777216 | tf_op jit(solution)/shard_map/psum | solution.py:82
  176.5 23.5 %collective-permute-start = (bf16[256,2048]{1,0:T(8,128)(2,1)S(1)}, bf16[256,2048]{1,0:T(8,128)(2,1)}, u32[]{:S(2)}, u32[]{:S(2)}) collective-permute-start(bf16[256,2048]{1,0:T(8,128)(2,1)S(1)} %convert_element_type.118), channel_id=1, source_target_pairs={{0,4},{4,0},{8,12},{12,8},{16,20},{20,16},{24,28},{28,24},{1,5},{5... | collective-permute-start | bytes 3145736 | tf_op jit(solution)/shard_map/ppermute | solution.py:20
  203.7 45.9 %collective-permute-start.1 = (bf16[512,2048]{1,0:T(8,128)(2,1)}, bf16[512,2048]{1,0:T(8,128)(2,1)}, u32[]{:S(2)}, u32[]{:S(2)}) collective-permute-start(bf16[512,2048]{1,0:T(8,128)(2,1)} %maximum_select_fusion.2), channel_id=1, source_target_pairs={{0,8},{4,12},{8,0},{12,4},{16,24},{20,28},{24,16},{28,20},{1,9},{5... | collective-permute-start | bytes 6291464 | tf_op jit(solution)/shard_map/ppermute | solution.py:20
  255.7 283.1 %collective-permute-start.2 = (bf16[1024,2048]{1,0:T(8,128)(2,1)}, bf16[1024,2048]{1,0:T(8,128)(2,1)}, u32[]{:S(2)}, u32[]{:S(2)}) collective-permute-start(bf16[1024,2048]{1,0:T(8,128)(2,1)} %maximum_select_fusion.1), channel_id=1, source_target_pairs={{0,16},{4,20},{8,24},{12,28},{16,0},{20,4},{24,8},{28,12},{1,17},{... | collective-permute-start | bytes 12582920 | tf_op jit(solution)/shard_map/ppermute | solution.py:20
  598.5 537.0 %all-reduce.10.cloned.1.call-start = ((), (), s32[]{:S(2)}) async-start(), calls=%async_computation.15 | async-start | bytes 33554432 | tf_op jit(solution)/shard_map/psum | solution.py:82
  846.4 289.2 %copy-start.27 = (f32[2048,1]{0,1:T(1,128)S(1)}, f32[2048,1]{0,1:T(1,128)}, u32[]{:S(2)}) copy-start(f32[2048,1]{0,1:T(1,128)} %copy-done.26) | copy-start | bytes 24580
  846.4 289.1 %copy-start.29 = (f32[1024]{0:T(1024)S(1)}, f32[1024]{0:T(1024)}, u32[]{:S(2)}) copy-start(f32[1024]{0:T(1024)} %copy-done.28) | copy-start | bytes 12292
  846.4 403.0 %reduce-scatter.10.cloned.1.call-start = ((), (), s32[]{:S(2)}) async-start(), calls=%async_computation.12 | async-start | bytes 4718592 | tf_op jit(solution)/shard_map/reduce_scatter | solution.py:238
  857.1 284.8 %copy-start.33 = (f32[1024]{0:T(1024)S(1)}, f32[1024]{0:T(1024)}, u32[]{:S(2)}) copy-start(f32[1024]{0:T(1024)} %copy-done.32) | copy-start | bytes 12292
  857.1 284.8 %copy-start.31 = (f32[1024]{0:T(1024)S(1)}, f32[1024]{0:T(1024)}, u32[]{:S(2)}) copy-start(f32[1024]{0:T(1024)} %copy-done.30) | copy-start | bytes 12292
  857.1 436.4 %reduce-scatter.6.cloned.1.call-start = ((), (), s32[]{:S(2)}) async-start(), calls=%async_computation.10 | async-start | bytes 73728 | tf_op jit(solution)/shard_map/reduce_scatter | solution.py:241
  1158.8 345.6 %reduce-scatter.8.cloned.1.call-start = ((), (), s32[]{:S(2)}) async-start(), calls=%async_computation.11 | async-start | bytes 14155776 | tf_op jit(solution)/shard_map/reduce_scatter | solution.py:237
  1172.6 617.0 %reduce-scatter.12.cloned.1.call-start = ((), (), s32[]{:S(2)}) async-start(), calls=%async_computation.13 | async-start | bytes 18874368 | tf_op jit(solution)/shard_map/reduce_scatter | solution.py:239
  1189.7 885.3 %reduce-scatter.14.cloned.1.call-start = ((), (), s32[]{:S(2)}) async-start(), calls=%async_computation.14 | async-start | bytes 18874368 | tf_op jit(solution)/shard_map/reduce_scatter | solution.py:240
  1207.1 872.0 %copy-start.34 = (f32[2048,1]{0,1:T(1,128)S(1)}, f32[2048,1]{0,1:T(1,128)}, u32[]{:S(2)}) copy-start(f32[2048,1]{0,1:T(1,128)} %get-tuple-element.119) | copy-start | bytes 24580
  (47 other events, 1049.4 us)
Sparse Core Ops, SparseCore 0:
  10.7 102.9 all-gather.3
  116.4 47.5 all-gather.5
  171.5 151.3 all-reduce.5
  325.4 183.7 all-gather.7
  598.6 175.0 all-reduce.7
  846.5 288.9 all-reduce.9
  1139.7 88.2 reduce-scatter.9
  1232.4 61.1 reduce-scatter.5
  1297.6 206.7 reduce-scatter.7
  1508.5 281.1 reduce-scatter.11
  1793.4 281.5 reduce-scatter.13
